TPU v7x, 32 devices: a whole 2x2x4 slice. The times are simulated.
32 devices in a mesh: box: 8 (over z, x), path: 4 (over y, core).
Axes of the slice: x: 2, y: 2, z: 4, core: 2. Of those that a mesh axis runs over, the one named last changes fastest.
Arguments:
- features: float32 [1024, 9, 128], P('box'), may hold values from -6 to 6
- positions: float32 [3, 1024], P(None, 'box'), may hold values from 0 to 96, as said below
- cotangent: bfloat16 [1024, 9, 128], P('box'), may hold values from -6 to 6
- weights: float32 [8, 8, 128], P('path'), may hold values from -2 to 2
- neighbours: int32 [16, 3], P('box'), may hold values from 0 to 3, as said below
- send_list: int32 [8, 2], P('box'), may hold values from 0 to 1, as said below
Outputs:
- grad_features: float32 [1024, 9, 128], P(('box', 'path'))
- grad_weights: float32 [8, 8, 128], P('path')
Inputs may be any that keep to these rules, and one draw needn't show every extreme that they name: `positions`: stored block s of box b has a place g = b * 2 + (a permutation of 0 to 1 within the box) along a chain; its atoms lie near the points of a grid of spacing 1.5 with 4 x 4 points across and 4 along the third coordinate, the first coordinate between 6 g and 6 g + 6, each moved by at most 0.35 in each coordinate. Blocks whose places differ by two or more have no atoms within 5 of each other. `neighbours`: row g lists the block itself (its stored index), the block one place before it and the block one place after it along the chain, as table indices: below 2 the box's own stored blocks, 2 the block received from the previous box (its last block along the chain), 3 the block received from the next box (its first block along the chain). The relation is symmetric. send_list[b, 0] is the stored index of the first block of box b's stretch of the chain and send_list[b, 1] that of the last.
All inputs are finite; a program needn't handle non-finite values.
Results may differ from a plain program's by a relative error of at most 0.0045.
Values may be sent and summed in bfloat16 or wider, within the bound.
A program may use at most 64 MiB of HBM per device.

v0:
```python
import math
import jax
import jax.numpy as jnp
from jax import lax
from jax.sharding import PartitionSpec as P

BASIS = 8
BLOCK = 64
NEIGHBOURS = 3
PATHS = 8
cutoff_radius = 5.0
edge_scale = 0.2
basis_width = 0.8
root_three = math.sqrt(3.0)
path_terms = [
    [(0, [(0, 0, 1.0)])],
    [(0, [(1, 1, 1.0), (2, 2, 1.0), (3, 3, 1.0)])],
    [(1, [(1, 0, 1.0)]), (2, [(2, 0, 1.0)]), (3, [(3, 0, 1.0)])],
    [(1, [(0, 1, 1.0)]), (2, [(0, 2, 1.0)]), (3, [(0, 3, 1.0)])],
    [
        (4, [(4, 0, 1.0)]),
        (5, [(5, 0, 1.0)]),
        (6, [(6, 0, 1.0)]),
        (7, [(7, 0, 1.0)]),
        (8, [(8, 0, 1.0)]),
    ],
    [
        (4, [(0, 4, 1.0)]),
        (5, [(0, 5, 1.0)]),
        (6, [(0, 6, 1.0)]),
        (7, [(0, 7, 1.0)]),
        (8, [(0, 8, 1.0)]),
    ],
    [
        (1, [(3, 2, 1.0), (2, 3, -1.0)]),
        (2, [(1, 3, 1.0), (3, 1, -1.0)]),
        (3, [(2, 1, 1.0), (1, 2, -1.0)]),
    ],
    [(0, [(4, 4, 1.0), (5, 5, 1.0), (6, 6, 1.0), (7, 7, 1.0), (8, 8, 1.0)])],
]


def with_halo(cells, sides, width):
    for axis, dim in sides:
        count = lax.axis_size(axis)
        ends = count - 1
        head = lax.slice_in_dim(cells, 0, width, axis=dim)
        tail = lax.slice_in_dim(cells, cells.shape[dim] - width, cells.shape[dim], axis=dim)
        cells = jnp.concatenate(
            [
                lax.ppermute(tail, axis, [(i, (i + 1) % count) for i in range(ends)]),
                cells,
                lax.ppermute(head, axis, [((i + 1) % count, i) for i in range(ends)]),
            ],
            axis=dim,
        )
    return cells


def edge_tensor(anchor, target):
    offset = target[:, None, :] - anchor[:, :, None]
    square = jnp.sum(offset * offset, axis=0)
    inside = square > 0.01
    distance = jnp.sqrt(jnp.where(inside, square, 1.0))
    direction = offset / distance[None]
    envelope = jnp.where(
        inside & (distance < cutoff_radius),
        0.5 * (jnp.cos(math.pi * distance / cutoff_radius) + 1.0),
        0.0,
    )
    centres = (jnp.arange(BASIS, dtype=jnp.float32) + 0.5) * (cutoff_radius / BASIS)
    radial = (
        jnp.exp(-jnp.square((distance[None] - centres[:, None, None]) / basis_width))
        * (edge_scale * envelope)[None]
    )
    eastward = direction[0]
    northward = direction[1]
    upward = direction[2]
    harmonics = jnp.stack(
        [
            jnp.ones_like(eastward),
            eastward,
            northward,
            upward,
            root_three * eastward * northward,
            root_three * northward * upward,
            0.5 * (3.0 * upward * upward - 1.0),
            root_three * eastward * upward,
            0.5 * root_three * (eastward * eastward - northward * northward),
        ]
    )
    return (harmonics[:, None] * radial[None]).astype(jnp.bfloat16)


def forward_terms(paths, weights, edge_table, rounded):
    source_rows = rounded.shape[0]
    target_rows = edge_table.shape[2]
    channels = rounded.shape[2]
    outputs = [jnp.zeros((target_rows, channels), jnp.float32) for output in range(9)]
    for weight_slot, path_number in enumerate(paths):
        for output, term_list in path_terms[path_number]:
            pieces = []
            stacked = []
            for harmonic, source, factor in term_list:
                signed = edge_table[harmonic] if factor > 0 else -edge_table[harmonic]
                pieces.append(signed.reshape(BASIS * target_rows, source_rows))
                stacked.append(rounded[:, source, :])
            product = jnp.dot(
                jnp.concatenate(pieces, axis=1),
                jnp.concatenate(stacked, axis=0),
                preferred_element_type=jnp.float32,
            )
            product = product.reshape(BASIS, target_rows, channels)
            outputs[output] = outputs[output] + jnp.sum(
                weights[weight_slot][:, None, :] * product, axis=0
            )
    return jnp.stack(outputs, axis=1)


def transpose_terms(paths, weights, edge_table, cotangent_rows, source_features):
    rows = source_features.shape[0]
    channels = source_features.shape[2]
    outputs = [jnp.zeros((rows, channels), jnp.float32) for output in range(9)]
    weight_parts = []
    for weight_slot, path_number in enumerate(paths):
        weight_part = jnp.zeros((BASIS, channels), jnp.float32)
        for output, term_list in path_terms[path_number]:
            for harmonic, source, factor in term_list:
                gathered = lax.dot_general(
                    edge_table[harmonic],
                    cotangent_rows[:, output, :],
                    (((1,), (0,)), ((), ())),
                    preferred_element_type=jnp.float32,
                )
                outputs[source] = outputs[source] + factor * jnp.sum(
                    weights[weight_slot][:, None, :] * gathered, axis=0
                )
                weight_part = weight_part + factor * jnp.sum(
                    source_features[:, source, :][None] * gathered, axis=1
                )
        weight_parts.append(weight_part)
    return (jnp.stack(outputs, axis=1), jnp.stack(weight_parts, axis=0))


def gate_back(message, cotangent):
    incoming = cotangent.astype(jnp.float32)
    scalar = message[:, 0]
    sigma = jax.nn.sigmoid(scalar)
    slope = sigma * (1.0 + scalar * (1.0 - sigma))
    coupling = jnp.sum(incoming[:, 1:] * message[:, 1:], axis=1)
    leading = incoming[:, 0] * slope + sigma * (1.0 - sigma) * coupling
    others = incoming[:, 1:] * sigma[:, None]
    return jnp.concatenate([leading[:, None], others], axis=1).astype(jnp.bfloat16)


def on_device(features, positions, cotangent, weights, neighbours, send_list):
    local_blocks = neighbours.shape[0]
    local_rows = features.shape[0]
    channels = features.shape[2]
    block_features = features.reshape(local_blocks, BLOCK, 9, channels)
    block_places = positions.reshape(3, local_blocks, BLOCK).transpose(1, 0, 2)
    outgoing = send_list[0]
    padded_features, padded_places = (
        with_halo(block_features[outgoing], (("box", 0),), 1),
        with_halo(block_places[outgoing], (("box", 0),), 1),
    )
    table_features = jnp.concatenate(
        [block_features, padded_features[:1], padded_features[3:]], axis=0
    )
    table_places = jnp.concatenate([block_places, padded_places[:1], padded_places[3:]], axis=0)
    table_rounded = table_features.astype(jnp.bfloat16)
    group = lax.axis_index("path")
    share_rows = local_rows // lax.axis_size("path")
    cotangent_share = lax.dynamic_slice_in_dim(cotangent, group * share_rows, share_rows, 0)
    all_weights = lax.all_gather(weights, "path", axis=0, tiled=True)
    all_paths = list(range(PATHS))
    slab_rows = math.gcd(share_rows, BLOCK)
    slab_numbers = jnp.arange(share_rows // slab_rows, dtype=jnp.int32)

    def slab_anchor(slab_index):
        first_row = group * share_rows + slab_index * slab_rows
        block_number = first_row // BLOCK
        within_row = first_row % BLOCK
        anchor_rows = lax.dynamic_slice_in_dim(block_places[block_number], within_row, slab_rows, 1)
        return (block_number, within_row, anchor_rows)

    def forward_slab(slab_index):
        block_number, within_row, anchor_rows = slab_anchor(slab_index)
        total = jnp.zeros((slab_rows, 9, channels), jnp.float32)
        for neighbour in range(NEIGHBOURS):
            table_slot = neighbours[block_number, neighbour]
            edge_table = edge_tensor(anchor_rows, table_places[table_slot])
            total = total + forward_terms(
                all_paths, all_weights, edge_table, table_rounded[table_slot]
            )
        return total

    message_rows = lax.map(forward_slab, slab_numbers).reshape(share_rows, 9, channels)
    gate_rows = gate_back(message_rows, cotangent_share)
    message_cotangent = lax.all_gather(gate_rows, "path", axis=0, tiled=True)
    cotangent_blocks = message_cotangent.reshape(local_blocks, BLOCK, 9, channels)
    padded_gate = with_halo(cotangent_blocks[outgoing], (("box", 0),), 1)
    table_gate = jnp.concatenate([cotangent_blocks, padded_gate[:1], padded_gate[3:]], axis=0)

    def pull_slab(slab_index):
        block_number, within_row, anchor_rows = slab_anchor(slab_index)
        own_features = lax.dynamic_slice_in_dim(
            block_features[block_number], within_row, slab_rows, 0
        )
        total = jnp.zeros((slab_rows, 9, channels), jnp.float32)
        weight_total = jnp.zeros((PATHS, BASIS, channels), jnp.float32)
        for neighbour in range(NEIGHBOURS):
            table_slot = neighbours[block_number, neighbour]
            edge_table = edge_tensor(table_places[table_slot], anchor_rows)
            contribution, weight_part = transpose_terms(
                all_paths, all_weights, edge_table, table_gate[table_slot], own_features
            )
            total = total + contribution
            weight_total = weight_total + weight_part
        return (total, weight_total)

    totals, slab_weights = lax.map(pull_slab, slab_numbers)
    grad_features = totals.reshape(share_rows, 9, channels) + cotangent_share.astype(jnp.float32)
    weight_every = lax.psum(jnp.sum(slab_weights, axis=0), ("box", "path"))
    group_paths = PATHS // lax.axis_size("path")
    weight_total = lax.dynamic_slice_in_dim(weight_every, group * group_paths, group_paths, 0)
    return (grad_features, weight_total / math.sqrt(local_rows * lax.axis_size("box")))


def solution(mesh):
    placed = (
        P("box", None, None),
        P(None, "box"),
        P("box", None, None),
        P("path", None, None),
        P("box", None),
        P("box", None),
    )
    return jax.shard_map(
        on_device,
        mesh=mesh,
        in_specs=placed,
        out_specs=(P(("box", "path"), None, None), P("path", None, None)),
        check_vma=False,
    )
```

profile of v0, /device:TPU:0, one launch (start us, length us, event | category | flops | bytes accessed | tf_op | source)
XLA Modules:
  0.0 147.7 jit_solution(1303785314537078605)
XLA Ops:
  0.6 0.8 reshape.2374
  1.4 0.7 fusion.347
  2.1 0.6 gather_fusion
  2.6 4.9 %collective-permute-start = (f32[1,3,64]{2,1,0:T(4,128)S(1)}, f32[1,3,64]{2,1,0:T(4,128)S(1)}, u32[]{:S(2)}, u32[]{:S(2)}) collective-permute-start(f32[1,3,64]{2,1,0:T(4,128)S(1)} %get-tuple-element.590), channel_id=1, source_target_pairs={{0,4},{4,8},{8,12},{12,16},{16,20},{20,24},{24,28},{1,5},{5,9},{9,... | collective-permute-start | bytes 2312 | tf_op jit(solution)/shard_map/ppermute | solution.py:51
  7.5 1.3 collective-permute-start.1
  8.8 1.7 %gather_fusion.1 = bf16[2,64,9,128]{3,1,2,0:T(8,128)(2,1)S(1)} fusion(f32[2,64,9,128]{3,1,0,2:T(8,128)} %bitcast.899, s32[1024]{0:T(1024)S(1)} %pad_clamp_fusion), kind=kCustom, calls=%fused_computation.1 | custom fusion | bytes 589832 | tf_op jit(solution)/shard_map/gather | solution.py:164
  10.5 0.7 fusion.388
  11.3 5.2 %collective-permute-start.2 = (bf16[1,64,9,128]{3,1,2,0:T(8,128)(2,1)}, bf16[1,64,9,128]{3,1,2,0:T(8,128)(2,1)}, u32[]{:S(2)}, u32[]{:S(2)}) collective-permute-start(bf16[1,64,9,128]{3,1,2,0:T(8,128)(2,1)} %get-tuple-element.509), channel_id=1, source_target_pairs={{0,4},{4,8},{8,12},{12,16},{16,20},{20,24},{24,28},{1,5},{5,9},{9,... | collective-permute-start | bytes 442376 | tf_op jit(solution)/shard_map/ppermute | solution.py:51
  16.5 1.3 collective-permute-start.3
  18.0 0.7 constant_dynamic-slice_fusion.3
  20.0 5.2 %all_gather.6 = f32[8,8,128]{2,1,0:T(8,128)S(1)} all-gather(f32[2,8,128]{2,1,0:T(8,128)S(1)} %copy-done.55), channel_id=1, replica_groups=mesh['box'=8,'path'=4] {'path'}, dimensions={0}, use_global_device_ids=true | all-gather | bytes 40960 | tf_op jit(solution)/shard_map/all_gather | solution.py:175
  25.2 0.6 slice_bitcast_fusion.210
  25.8 0.7 slice_bitcast_fusion.96
  26.4 1.6 %dynamic-slice_convert_fusion = f32[32,9,128]{2,0,1:T(8,128)} fusion(bf16[128,9,128]{2,0,1:T(8,128)(2,1)} %param.8, s32[]{:T(128)S(6)} %select_n.212), kind=kLoop, calls=%fused_computation.489 | loop fusion | flops 36864 | bytes 221188 | tf_op jit(solution)/shard_map/convert_element_type | solution.py:146
  33.4 0.8 fusion.384
  34.3 0.7 fusion.385
  35.3 0.8 fusion.386
  36.1 0.7 bitcast_negate_fusion.7
  36.8 0.6 bitcast_negate_fusion.2
  37.4 0.6 bitcast_negate_fusion
  38.1 0.6 bitcast_negate_fusion.1
  38.7 0.7 bitcast_negate_fusion.3
  39.4 0.7 bitcast_negate_fusion.4
  40.0 0.6 bitcast_negate_fusion.8
  40.6 0.6 bitcast_negate_fusion.6
  42.0 0.5 copy-done.32
  42.8 0.8 copy-done.33
  43.7 1.8 %concatenate.157 = bf16[256,320]{1,0:T(8,128)(2,1)} concatenate(bf16[256,64]{1,0:T(8,128)(2,1)} %bitcast.946, bf16[256,64]{1,0:T(8,128)(2,1)} %bitcast.945, bf16[256,64]{1,0:T(8,128)(2,1)} %bitcast.944, bf16[256,64]{1,0:T(8,128)(2,1)} %bitcast.943, bf16[256,64]{1,0:T(8,128)(2,1)} %bitcast.942), dimensions={1} | concatenate | bytes 327680 | tf_op jit(solution)/shard_map/while/body/eval_jaxpr/concatenate | solution.py:109
  45.4 1.8 %concatenate.167 = bf16[256,320]{1,0:T(8,128)(2,1)} concatenate(bf16[256,64]{1,0:T(8,128)(2,1)} %bitcast.941, bf16[256,64]{1,0:T(8,128)(2,1)} %bitcast.940, bf16[256,64]{1,0:T(8,128)(2,1)} %bitcast.939, bf16[256,64]{1,0:T(8,128)(2,1)} %bitcast.938, bf16[256,64]{1,0:T(8,128)(2,1)} %bitcast.937), dimensions={1} | concatenate | bytes 327680 | tf_op jit(solution)/shard_map/while/body/eval_jaxpr/concatenate | solution.py:109
  47.2 1.8 %concatenate.147 = bf16[256,320]{1,0:T(8,128)(2,1)} concatenate(bf16[256,64]{1,0:T(8,128)(2,1)} %bitcast.936, bf16[256,64]{1,0:T(8,128)(2,1)} %bitcast.935, bf16[256,64]{1,0:T(8,128)(2,1)} %bitcast.934, bf16[256,64]{1,0:T(8,128)(2,1)} %bitcast.933, bf16[256,64]{1,0:T(8,128)(2,1)} %bitcast.932), dimensions={1} | concatenate | bytes 327680 | tf_op jit(solution)/shard_map/while/body/eval_jaxpr/concatenate | solution.py:109
  49.0 0.8 bitcast_negate_fusion.5
  49.8 1.1 pad_maximum_fusion
  51.1 0.9 copy-done.2
  60.0 0.2 fusion.102
  60.2 0.2 fusion.64
  60.9 0.2 fusion.94
  61.1 0.2 fusion.86
  61.4 0.2 fusion.58
  62.2 0.2 fusion.52
  62.6 0.2 fusion.78
  62.8 0.2 fusion.74
  63.8 0.3 copy-done.6
  64.9 0.7 copy-done.3
  65.7 6.0 %all_gather.7 = bf16[128,9,128]{2,0,1:T(8,128)(2,1)S(1)} all-gather(bf16[32,9,128]{2,0,1:T(8,128)(2,1)S(1)} %pad_maximum_fusion.1), channel_id=1, replica_groups=mesh['box'=8,'path'=4] {'path'}, dimensions={0}, use_global_device_ids=true | all-gather | bytes 368640 | tf_op jit(solution)/shard_map/all_gather | solution.py:200
  71.8 0.7 gather_fusion.2
  72.5 4.6 %collective-permute-start.4 = (bf16[1,64,9,128]{3,1,2,0:T(8,128)(2,1)S(1)}, bf16[1,64,9,128]{3,1,2,0:T(8,128)(2,1)S(1)}, u32[]{:S(2)}, u32[]{:S(2)}) collective-permute-start(bf16[1,64,9,128]{3,1,2,0:T(8,128)(2,1)S(1)} %get-tuple-element.508), channel_id=1, source_target_pairs={{0,4},{4,8},{8,12},{12,16},{16,20},{20,24},{24,28},{1,5},{5,9},{9,... | collective-permute-start | bytes 442376 | tf_op jit(solution)/shard_map/ppermute | solution.py:51
  77.1 1.5 collective-permute-start.5
  78.6 2.1 %collective-permute-done.4 = bf16[1,64,9,128]{3,1,2,0:T(8,128)(2,1)S(1)} collective-permute-done((bf16[1,64,9,128]{3,1,2,0:T(8,128)(2,1)S(1)}, bf16[1,64,9,128]{3,1,2,0:T(8,128)(2,1)S(1)}, u32[]{:S(2)}, u32[]{:S(2)}) %collective-permute-start.4) | collective-permute-done | bytes 147488 | tf_op jit(solution)/shard_map/ppermute | solution.py:51
  80.7 5.1 %collective-permute-done.5 = bf16[1,64,9,128]{3,1,2,0:T(8,128)(2,1)S(1)} collective-permute-done((bf16[1,64,9,128]{3,1,2,0:T(8,128)(2,1)S(1)}, bf16[1,64,9,128]{3,1,2,0:T(8,128)(2,1)S(1)}, u32[]{:S(2)}, u32[]{:S(2)}) %collective-permute-start.5) | collective-permute-done | bytes 147488 | tf_op jit(solution)/shard_map/ppermute | solution.py:53
  98.1 0.4 multiply_reduce_fusion.24
  98.5 0.2 copy-done.40
  98.8 0.4 multiply_reduce_fusion.8
  99.2 0.3 copy-done.47
  99.5 0.4 multiply_reduce_fusion.5
  99.9 0.3 copy-done.46
  100.2 0.4 multiply_reduce_fusion.6
  100.9 0.5 multiply_reduce_fusion.16
  101.8 0.2 copy-done.43
  102.1 0.3 multiply_reduce_fusion.1
  102.4 0.4 copy-done.41
  102.8 0.3 multiply_reduce_fusion
  103.4 41.7 %psum.7 = f32[8,8,128]{2,1,0:T(8,128)S(1)} all-reduce(f32[8,8,128]{2,1,0:T(8,128)S(1)} %add_add_fusion.2), channel_id=1, replica_groups=mesh['box'=8,'path'=4] {'box','path'}, use_global_device_ids=true, to_apply=%region_259.260 | all-reduce | flops 8192 | bytes 65536 | tf_op jit(solution)/shard_map/psum | solution.py:224
  145.1 0.6 dynamic-slice_multiply_fusion
  146.1 1.6 %add_add_fusion = f32[32,9,128]{2,0,1:T(8,128)} fusion(f32[32,9,128]{2,0,1:T(8,128)S(1)} %constant_dynamic-update-slice_fusion.104, f32[32,9,128]{2,0,1:T(8,128)S(1)} %constant_dynamic-update-slice_fusion.72, f32[32,9,128]{2,0,1:T(8,128)S(1)} %constant_dynamic-update-slice_fusion.88, bf16[128,9,128]{2,0,1:T(8,128)(2,1)} %param.8, s32[]{:T(128)S(6)} %select_n.212), kind=kLoop, calls=%fused_computation.252 | loop fusion | flops 147456 | bytes 663556 | tf_op jit(solution)/shard_map/add | solution.py:223
  (425 shorter events, 25.2 us)
Async XLA Ops:
  2.1 9.2 %copy-start.56 = (s32[1024]{0:T(1024)}, s32[1024]{0:T(1024)S(1)}, u32[]{:S(2)}) copy-start(s32[1024]{0:T(1024)S(1)} %pad_clamp_fusion) | copy-start | bytes 12292
  2.6 29.8 %collective-permute-start = (f32[1,3,64]{2,1,0:T(4,128)S(1)}, f32[1,3,64]{2,1,0:T(4,128)S(1)}, u32[]{:S(2)}, u32[]{:S(2)}) collective-permute-start(f32[1,3,64]{2,1,0:T(4,128)S(1)} %get-tuple-element.590), channel_id=1, source_target_pairs={{0,4},{4,8},{8,12},{12,16},{16,20},{20,24},{24,28},{1,5},{5,9},{9,... | collective-permute-start | bytes 2312 | tf_op jit(solution)/shard_map/ppermute | solution.py:51
  7.5 24.9 %collective-permute-start.1 = (f32[1,3,64]{2,1,0:T(4,128)S(1)}, f32[1,3,64]{2,1,0:T(4,128)S(1)}, u32[]{:S(2)}, u32[]{:S(2)}) collective-permute-start(f32[1,3,64]{2,1,0:T(4,128)S(1)} %get-tuple-element.591), channel_id=1, source_target_pairs={{4,0},{8,4},{12,8},{16,12},{20,16},{24,20},{28,24},{5,1},{9,5},{13... | collective-permute-start | bytes 2312 | tf_op jit(solution)/shard_map/ppermute | solution.py:53
  10.5 7.5 %copy-start = (f32[128,9,128]{2,0,1:T(8,128)S(1)}, f32[128,9,128]{2,0,1:T(8,128)}, u32[]{:S(2)}) copy-start(f32[128,9,128]{2,0,1:T(8,128)} %param.6) | copy-start | bytes 1769476
  10.5 7.5 %copy-start.57 = (s32[2,3]{1,0:T(2,128)S(1)}, s32[2,3]{1,0:T(2,128)}, u32[]{:S(2)}) copy-start(s32[2,3]{1,0:T(2,128)} %param.10) | copy-start | bytes 76
  10.5 9.5 %copy-start.55 = (f32[2,8,128]{2,1,0:T(8,128)S(1)}, f32[2,8,128]{2,1,0:T(8,128)}, u32[]{:S(2)}) copy-start(f32[2,8,128]{2,1,0:T(8,128)} %param.9) | copy-start | bytes 24580
  11.3 38.5 %collective-permute-start.2 = (bf16[1,64,9,128]{3,1,2,0:T(8,128)(2,1)}, bf16[1,64,9,128]{3,1,2,0:T(8,128)(2,1)}, u32[]{:S(2)}, u32[]{:S(2)}) collective-permute-start(bf16[1,64,9,128]{3,1,2,0:T(8,128)(2,1)} %get-tuple-element.509), channel_id=1, source_target_pairs={{0,4},{4,8},{8,12},{12,16},{16,20},{20,24},{24,28},{1,5},{5,9},{9,... | collective-permute-start | bytes 442376 | tf_op jit(solution)/shard_map/ppermute | solution.py:51
  16.5 33.4 %collective-permute-start.3 = (bf16[1,64,9,128]{3,1,2,0:T(8,128)(2,1)}, bf16[1,64,9,128]{3,1,2,0:T(8,128)(2,1)}, u32[]{:S(2)}, u32[]{:S(2)}) collective-permute-start(bf16[1,64,9,128]{3,1,2,0:T(8,128)(2,1)} %get-tuple-element.510), channel_id=1, source_target_pairs={{4,0},{8,4},{12,8},{16,12},{20,16},{24,20},{28,24},{5,1},{9,5},{13... | collective-permute-start | bytes 442376 | tf_op jit(solution)/shard_map/ppermute | solution.py:53
  34.1 2.0 %copy-start.9 = (bf16[1,8,32,64]{3,2,1,0:T(8,128)(2,1)}, bf16[1,8,32,64]{3,2,1,0:T(8,128)(2,1)S(1)}, u32[]{:S(2)}) copy-start(bf16[1,8,32,64]{3,2,1,0:T(8,128)(2,1)S(1)} %get-tuple-element.487) | copy-start | bytes 98308
  34.1 5.9 %copy-start.7 = (bf16[1,8,32,64]{3,2,1,0:T(8,128)(2,1)}, bf16[1,8,32,64]{3,2,1,0:T(8,128)(2,1)S(1)}, u32[]{:S(2)}) copy-start(bf16[1,8,32,64]{3,2,1,0:T(8,128)(2,1)S(1)} %get-tuple-element.480) | copy-start | bytes 98308
  34.1 6.5 %copy-start.11 = (bf16[1,8,32,64]{3,2,1,0:T(8,128)(2,1)}, bf16[1,8,32,64]{3,2,1,0:T(8,128)(2,1)S(1)}, u32[]{:S(2)}) copy-start(bf16[1,8,32,64]{3,2,1,0:T(8,128)(2,1)S(1)} %get-tuple-element.486) | copy-start | bytes 98308
  35.1 1.7 %copy-start.17 = (bf16[1,8,32,64]{3,2,1,0:T(8,128)(2,1)}, bf16[1,8,32,64]{3,2,1,0:T(8,128)(2,1)S(1)}, u32[]{:S(2)}) copy-start(bf16[1,8,32,64]{3,2,1,0:T(8,128)(2,1)S(1)} %get-tuple-element.488) | copy-start | bytes 98308
  35.1 2.3 %copy-start.15 = (bf16[1,8,32,64]{3,2,1,0:T(8,128)(2,1)}, bf16[1,8,32,64]{3,2,1,0:T(8,128)(2,1)S(1)}, u32[]{:S(2)}) copy-start(bf16[1,8,32,64]{3,2,1,0:T(8,128)(2,1)S(1)} %get-tuple-element.494) | copy-start | bytes 98308
  35.1 3.0 %copy-start.19 = (bf16[1,8,32,64]{3,2,1,0:T(8,128)(2,1)}, bf16[1,8,32,64]{3,2,1,0:T(8,128)(2,1)S(1)}, u32[]{:S(2)}) copy-start(bf16[1,8,32,64]{3,2,1,0:T(8,128)(2,1)S(1)} %get-tuple-element.495) | copy-start | bytes 98308
  35.3 1.5 %copy-start.1 = (bf16[9,8,32,64]{3,2,1,0:T(8,128)(2,1)}, bf16[9,8,32,64]{3,2,1,0:T(8,128)(2,1)S(1)}, u32[]{:S(2)}) copy-start(bf16[9,8,32,64]{3,2,1,0:T(8,128)(2,1)S(1)} %multiply_convert_fusion.3) | copy-start | bytes 884740
  36.1 5.4 %copy-start.13 = (bf16[1,8,32,64]{3,2,1,0:T(8,128)(2,1)}, bf16[1,8,32,64]{3,2,1,0:T(8,128)(2,1)S(1)}, u32[]{:S(2)}) copy-start(bf16[1,8,32,64]{3,2,1,0:T(8,128)(2,1)S(1)} %get-tuple-element.503) | copy-start | bytes 98308
  36.1 5.4 %copy-start.21 = (bf16[1,8,32,64]{3,2,1,0:T(8,128)(2,1)}, bf16[1,8,32,64]{3,2,1,0:T(8,128)(2,1)S(1)}, u32[]{:S(2)}) copy-start(bf16[1,8,32,64]{3,2,1,0:T(8,128)(2,1)S(1)} %get-tuple-element.502) | copy-start | bytes 98308
  41.9 0.7 copy-start.32
  42.6 0.9 copy-start.33
  50.9 1.1 copy-start.2
  50.9 1.1 copy-start.51
  50.9 1.3 copy-start.39
  51.0 1.9 %copy-start.49 = (f32[8,128]{1,0:T(8,128)S(1)}, f32[8,128]{1,0:T(8,128)}, u32[]{:S(2)}) copy-start(f32[8,128]{1,0:T(8,128)} %get-tuple-element.532) | copy-start | bytes 12292
  52.0 1.2 copy-start.37
  53.2 1.2 copy-start.53
  59.0 1.0 copy-start.20
  59.0 1.0 copy-start.31
  59.3 0.9 copy-start.16
  59.3 0.9 copy-start.18
  59.8 0.9 copy-start.30
  59.9 1.0 copy-start.29
  60.2 0.9 copy-start.23
  60.2 0.9 copy-start.28
  60.2 1.1 copy-start.14
  60.2 1.1 copy-start.22
  60.9 0.9 copy-start.27
  61.1 0.9 copy-start.12
  61.1 0.9 copy-start.25
  61.3 0.9 copy-start.8
  61.3 0.9 copy-start.10
  61.7 0.9 copy-start.26
  61.9 0.9 copy-start.24
  62.2 1.0 copy-start.4
  62.6 1.0 copy-start.5
  63.0 1.0 copy-start.6
  63.3 0.9 copy-start.36
  63.6 0.7 copy-start.34
  63.6 0.7 copy-start.35
  64.7 0.9 copy-start.3
  72.5 8.2 %collective-permute-start.4 = (bf16[1,64,9,128]{3,1,2,0:T(8,128)(2,1)S(1)}, bf16[1,64,9,128]{3,1,2,0:T(8,128)(2,1)S(1)}, u32[]{:S(2)}, u32[]{:S(2)}) collective-permute-start(bf16[1,64,9,128]{3,1,2,0:T(8,128)(2,1)S(1)} %get-tuple-element.508), channel_id=1, source_target_pairs={{0,4},{4,8},{8,12},{12,16},{16,20},{20,24},{24,28},{1,5},{5,9},{9,... | collective-permute-start | bytes 442376 | tf_op jit(solution)/shard_map/ppermute | solution.py:51
  77.1 8.7 %collective-permute-start.5 = (bf16[1,64,9,128]{3,1,2,0:T(8,128)(2,1)S(1)}, bf16[1,64,9,128]{3,1,2,0:T(8,128)(2,1)S(1)}, u32[]{:S(2)}, u32[]{:S(2)}) collective-permute-start(bf16[1,64,9,128]{3,1,2,0:T(8,128)(2,1)S(1)} %get-tuple-element.507), channel_id=1, source_target_pairs={{4,0},{8,4},{12,8},{16,12},{20,16},{24,20},{28,24},{5,1},{9,5},{13... | collective-permute-start | bytes 442376 | tf_op jit(solution)/shard_map/ppermute | solution.py:53
  97.1 0.9 copy-start.52
  97.2 0.9 copy-start.54
  98.0 0.7 copy-start.40
  98.1 0.7 copy-start.48
  98.8 0.7 copy-start.47
  99.5 0.7 copy-start.46
  100.2 0.7 copy-start.50
  100.9 0.7 copy-start.38
  100.9 0.7 copy-start.45
  101.4 0.7 copy-start.43
  101.4 0.7 copy-start.44
  102.1 0.7 copy-start.41
  102.1 0.7 copy-start.42
where the time goes:
time: 149 us; the launch traced here: 148 us
  blocking collectives  53 us (36%)
  matrix products  25 us (17%)
  local copies, waits for them, and re-layouts  20.3 us (14%)
  starting transfers between devices  18.7 us (13%)
  other arithmetic  14.5 us (10%)
  between operations  9.16 us (6%)
  waiting for transfers between devices  7.16 us (5%)
    psum x1, blocking collectives, on_device(): weight_every = lax.psum(jnp.sum(slab_weights, axis=0), ('box', 'path'))  41.7 us
    ppermute x3, starting transfers between devices, with_halo(): lax.ppermute(tail, axis, [(i, (i + 1) % count) for i in range(ends)])  14.6 us
    dot_general x93, matrix products, transpose_terms(): lax.dot_general(edge_table[harmonic], cotangent_rows[:, output, :], (((1,...  14.4 us
    dot_general x66, matrix products, forward_terms(): jnp.dot(jnp.concatenate(pieces, axis=1), jnp.concatenate(stacked, axis=0)...  10.6 us
    all_gather x1, blocking collectives, on_device(): message_cotangent = lax.all_gather(gate_rows, 'path', axis=0, tiled=True)  6.04 us
    unnamed x139, local copies, waits for them, and re-layouts  6.02 us
    neg x9, other arithmetic, forward_terms(): signed = edge_table[harmonic] if factor > 0 else -edge_table[harmonic]  6.01 us
    concatenate x3, local copies, waits for them, and re-layouts, forward_terms(): jnp.concatenate(pieces, axis=1)  5.3 us
  transfers between devices with their start and end apart: 6, of which 2 were waited for; matrix products, arithmetic and copies ran while one was open for 15% of the time, Pallas kernels for 0%

commit v1 on v0

--- a/solution.py
+++ b/solution.py
@@ -221,7 +221,7 @@
 
     totals, slab_weights = lax.map(pull_slab, slab_numbers)
     grad_features = totals.reshape(share_rows, 9, channels) + cotangent_share.astype(jnp.float32)
-    weight_every = lax.psum(jnp.sum(slab_weights, axis=0), ("box", "path"))
+    weight_every = lax.psum(lax.psum(jnp.sum(slab_weights, axis=0), "path"), "box")
     group_paths = PATHS // lax.axis_size("path")
     weight_total = lax.dynamic_slice_in_dim(weight_every, group * group_paths, group_paths, 0)
     return (grad_features, weight_total / math.sqrt(local_rows * lax.axis_size("box")))

time: 149 us -> 155 us (1.040)
  blocking collectives: 53 us -> 59.2 us
    psum x1 -> x2, blocking collectives: 41.7 us -> 48 us  [the longest x1 37.2 us: on_device(): lax.psum(lax.psum(jnp.sum(slab_weights, axis=0), 'path'), 'box')]
  transfers between devices with their start and end apart: 6 -> 6, of which waited for: 2 -> 2; matrix products, arithmetic and copies ran while one was open for 15% -> 14% of each run, Pallas kernels for 0% -> 0%
where the time goes in v1:
time: 155 us; the launch traced here: 154 us
  blocking collectives  59.2 us (38%)
  matrix products  25 us (16%)
  local copies, waits for them, and re-layouts  20.3 us (13%)
  starting transfers between devices  18.7 us (12%)
  other arithmetic  14.4 us (9%)
  between operations  9.16 us (6%)
  waiting for transfers between devices  7.16 us (5%)
    psum x1, blocking collectives, on_device(): lax.psum(lax.psum(jnp.sum(slab_weights, axis=0), 'path'), 'box')  37.2 us
    ppermute x3, starting transfers between devices, with_halo(): lax.ppermute(tail, axis, [(i, (i + 1) % count) for i in range(ends)])  14.6 us
    dot_general x93, matrix products, transpose_terms(): lax.dot_general(edge_table[harmonic], cotangent_rows[:, output, :], (((1,...  14.4 us
    psum x1, blocking collectives, on_device(): lax.psum(jnp.sum(slab_weights, axis=0), 'path')  10.8 us
    dot_general x66, matrix products, forward_terms(): jnp.dot(jnp.concatenate(pieces, axis=1), jnp.concatenate(stacked, axis=0)...  10.6 us
    all_gather x1, blocking collectives, on_device(): message_cotangent = lax.all_gather(gate_rows, 'path', axis=0, tiled=True)  6.04 us
    unnamed x139, local copies, waits for them, and re-layouts  6.02 us
    neg x9, other arithmetic, forward_terms(): signed = edge_table[harmonic] if factor > 0 else -edge_table[harmonic]  6.01 us
  transfers between devices with their start and end apart: 6, of which 2 were waited for; matrix products, arithmetic and copies ran while one was open for 14% of the time, Pallas kernels for 0%

profile of v1, /device:TPU:0, one launch (start us, length us, event | category | flops | bytes accessed | tf_op | source)
XLA Modules:
  0.0 153.9 jit_solution(14197606802374449305)
XLA Ops:
  0.6 0.8 reshape.2374
  1.4 0.7 fusion.347
  2.1 0.6 gather_fusion
  2.6 4.9 %collective-permute-start = (f32[1,3,64]{2,1,0:T(4,128)S(1)}, f32[1,3,64]{2,1,0:T(4,128)S(1)}, u32[]{:S(2)}, u32[]{:S(2)}) collective-permute-start(f32[1,3,64]{2,1,0:T(4,128)S(1)} %get-tuple-element.590), channel_id=1, source_target_pairs={{0,4},{4,8},{8,12},{12,16},{16,20},{20,24},{24,28},{1,5},{5,9},{9,... | collective-permute-start | bytes 2312 | tf_op jit(solution)/shard_map/ppermute | solution.py:51
  7.5 1.3 collective-permute-start.1
  8.8 1.7 %gather_fusion.1 = bf16[2,64,9,128]{3,1,2,0:T(8,128)(2,1)S(1)} fusion(f32[2,64,9,128]{3,1,0,2:T(8,128)} %bitcast.899, s32[1024]{0:T(1024)S(1)} %pad_clamp_fusion), kind=kCustom, calls=%fused_computation.1 | custom fusion | bytes 589832 | tf_op jit(solution)/shard_map/gather | solution.py:164
  10.5 0.7 fusion.388
  11.3 5.2 %collective-permute-start.2 = (bf16[1,64,9,128]{3,1,2,0:T(8,128)(2,1)}, bf16[1,64,9,128]{3,1,2,0:T(8,128)(2,1)}, u32[]{:S(2)}, u32[]{:S(2)}) collective-permute-start(bf16[1,64,9,128]{3,1,2,0:T(8,128)(2,1)} %get-tuple-element.509), channel_id=1, source_target_pairs={{0,4},{4,8},{8,12},{12,16},{16,20},{20,24},{24,28},{1,5},{5,9},{9,... | collective-permute-start | bytes 442376 | tf_op jit(solution)/shard_map/ppermute | solution.py:51
  16.5 1.3 collective-permute-start.3
  18.0 0.7 constant_dynamic-slice_fusion.3
  20.0 5.2 %all_gather.6 = f32[8,8,128]{2,1,0:T(8,128)S(1)} all-gather(f32[2,8,128]{2,1,0:T(8,128)S(1)} %copy-done.55), channel_id=1, replica_groups=mesh['box'=8,'path'=4] {'path'}, dimensions={0}, use_global_device_ids=true | all-gather | bytes 40960 | tf_op jit(solution)/shard_map/all_gather | solution.py:175
  25.2 0.6 slice_bitcast_fusion.210
  25.8 0.7 slice_bitcast_fusion.96
  26.4 1.6 %dynamic-slice_convert_fusion = f32[32,9,128]{2,0,1:T(8,128)} fusion(bf16[128,9,128]{2,0,1:T(8,128)(2,1)} %param.8, s32[]{:T(128)S(6)} %select_n.212), kind=kLoop, calls=%fused_computation.489 | loop fusion | flops 36864 | bytes 221188 | tf_op jit(solution)/shard_map/convert_element_type | solution.py:146
  33.4 0.8 fusion.384
  34.3 0.7 fusion.385
  35.3 0.8 fusion.386
  36.1 0.7 bitcast_negate_fusion.7
  36.8 0.6 bitcast_negate_fusion.2
  37.4 0.6 bitcast_negate_fusion
  38.1 0.6 bitcast_negate_fusion.1
  38.7 0.7 bitcast_negate_fusion.3
  39.4 0.7 bitcast_negate_fusion.4
  40.0 0.6 bitcast_negate_fusion.8
  40.6 0.6 bitcast_negate_fusion.6
  42.0 0.5 copy-done.32
  42.8 0.8 copy-done.33
  43.7 1.8 %concatenate.157 = bf16[256,320]{1,0:T(8,128)(2,1)} concatenate(bf16[256,64]{1,0:T(8,128)(2,1)} %bitcast.946, bf16[256,64]{1,0:T(8,128)(2,1)} %bitcast.945, bf16[256,64]{1,0:T(8,128)(2,1)} %bitcast.944, bf16[256,64]{1,0:T(8,128)(2,1)} %bitcast.943, bf16[256,64]{1,0:T(8,128)(2,1)} %bitcast.942), dimensions={1} | concatenate | bytes 327680 | tf_op jit(solution)/shard_map/while/body/eval_jaxpr/concatenate | solution.py:109
  45.4 1.8 %concatenate.167 = bf16[256,320]{1,0:T(8,128)(2,1)} concatenate(bf16[256,64]{1,0:T(8,128)(2,1)} %bitcast.941, bf16[256,64]{1,0:T(8,128)(2,1)} %bitcast.940, bf16[256,64]{1,0:T(8,128)(2,1)} %bitcast.939, bf16[256,64]{1,0:T(8,128)(2,1)} %bitcast.938, bf16[256,64]{1,0:T(8,128)(2,1)} %bitcast.937), dimensions={1} | concatenate | bytes 327680 | tf_op jit(solution)/shard_map/while/body/eval_jaxpr/concatenate | solution.py:109
  47.2 1.8 %concatenate.147 = bf16[256,320]{1,0:T(8,128)(2,1)} concatenate(bf16[256,64]{1,0:T(8,128)(2,1)} %bitcast.936, bf16[256,64]{1,0:T(8,128)(2,1)} %bitcast.935, bf16[256,64]{1,0:T(8,128)(2,1)} %bitcast.934, bf16[256,64]{1,0:T(8,128)(2,1)} %bitcast.933, bf16[256,64]{1,0:T(8,128)(2,1)} %bitcast.932), dimensions={1} | concatenate | bytes 327680 | tf_op jit(solution)/shard_map/while/body/eval_jaxpr/concatenate | solution.py:109
  49.0 0.8 bitcast_negate_fusion.5
  49.8 1.1 pad_maximum_fusion
  51.1 0.9 copy-done.2
  60.0 0.2 fusion.102
  60.2 0.2 fusion.64
  60.9 0.2 fusion.94
  61.1 0.2 fusion.86
  61.4 0.2 fusion.58
  62.2 0.2 fusion.52
  62.8 0.2 fusion.74
  63.8 0.3 copy-done.6
  64.9 0.7 copy-done.3
  65.7 6.0 %all_gather.7 = bf16[128,9,128]{2,0,1:T(8,128)(2,1)S(1)} all-gather(bf16[32,9,128]{2,0,1:T(8,128)(2,1)S(1)} %pad_maximum_fusion.1), channel_id=1, replica_groups=mesh['box'=8,'path'=4] {'path'}, dimensions={0}, use_global_device_ids=true | all-gather | bytes 368640 | tf_op jit(solution)/shard_map/all_gather | solution.py:200
  71.8 0.7 gather_fusion.2
  72.5 4.6 %collective-permute-start.4 = (bf16[1,64,9,128]{3,1,2,0:T(8,128)(2,1)S(1)}, bf16[1,64,9,128]{3,1,2,0:T(8,128)(2,1)S(1)}, u32[]{:S(2)}, u32[]{:S(2)}) collective-permute-start(bf16[1,64,9,128]{3,1,2,0:T(8,128)(2,1)S(1)} %get-tuple-element.508), channel_id=1, source_target_pairs={{0,4},{4,8},{8,12},{12,16},{16,20},{20,24},{24,28},{1,5},{5,9},{9,... | collective-permute-start | bytes 442376 | tf_op jit(solution)/shard_map/ppermute | solution.py:51
  77.1 1.5 collective-permute-start.5
  78.6 2.1 %collective-permute-done.4 = bf16[1,64,9,128]{3,1,2,0:T(8,128)(2,1)S(1)} collective-permute-done((bf16[1,64,9,128]{3,1,2,0:T(8,128)(2,1)S(1)}, bf16[1,64,9,128]{3,1,2,0:T(8,128)(2,1)S(1)}, u32[]{:S(2)}, u32[]{:S(2)}) %collective-permute-start.4) | collective-permute-done | bytes 147488 | tf_op jit(solution)/shard_map/ppermute | solution.py:51
  80.7 5.1 %collective-permute-done.5 = bf16[1,64,9,128]{3,1,2,0:T(8,128)(2,1)S(1)} collective-permute-done((bf16[1,64,9,128]{3,1,2,0:T(8,128)(2,1)S(1)}, bf16[1,64,9,128]{3,1,2,0:T(8,128)(2,1)S(1)}, u32[]{:S(2)}, u32[]{:S(2)}) %collective-permute-start.5) | collective-permute-done | bytes 147488 | tf_op jit(solution)/shard_map/ppermute | solution.py:53
  98.1 0.4 multiply_reduce_fusion.24
  98.5 0.2 copy-done.40
  98.8 0.4 multiply_reduce_fusion.8
  99.2 0.3 copy-done.47
  99.5 0.4 multiply_reduce_fusion.5
  99.9 0.3 copy-done.46
  100.2 0.4 multiply_reduce_fusion.6
  100.9 0.5 multiply_reduce_fusion.16
  101.8 0.2 copy-done.43
  102.1 0.3 multiply_reduce_fusion.1
  102.4 0.4 copy-done.41
  102.8 0.3 multiply_reduce_fusion
  103.4 10.8 %psum.14 = f32[8,8,128]{2,1,0:T(8,128)S(1)} all-reduce(f32[8,8,128]{2,1,0:T(8,128)S(1)} %add_add_fusion.2), channel_id=1, replica_groups=mesh['box'=8,'path'=4] {'path'}, use_global_device_ids=true, to_apply=%region_259.260 | all-reduce | flops 8192 | bytes 65536 | tf_op jit(solution)/shard_map/psum | solution.py:224
  114.1 37.2 %psum.15 = f32[8,8,128]{2,1,0:T(8,128)S(1)} all-reduce(f32[8,8,128]{2,1,0:T(8,128)S(1)} %psum.14), channel_id=1, replica_groups=mesh['box'=8,'path'=4] {'box'}, use_global_device_ids=true, to_apply=%region_260.261 | all-reduce | flops 8192 | bytes 65536 | tf_op jit(solution)/shard_map/psum | solution.py:224
  151.3 0.6 dynamic-slice_multiply_fusion
  152.3 1.6 %add_add_fusion = f32[32,9,128]{2,0,1:T(8,128)} fusion(f32[32,9,128]{2,0,1:T(8,128)S(1)} %constant_dynamic-update-slice_fusion.104, f32[32,9,128]{2,0,1:T(8,128)S(1)} %constant_dynamic-update-slice_fusion.72, f32[32,9,128]{2,0,1:T(8,128)S(1)} %constant_dynamic-update-slice_fusion.88, bf16[128,9,128]{2,0,1:T(8,128)(2,1)} %param.8, s32[]{:T(128)S(6)} %select_n.212), kind=kLoop, calls=%fused_computation.252 | loop fusion | flops 147456 | bytes 663556 | tf_op jit(solution)/shard_map/add | solution.py:223
  (426 shorter events, 25.4 us)
Async XLA Ops:
  2.1 9.2 %copy-start.56 = (s32[1024]{0:T(1024)}, s32[1024]{0:T(1024)S(1)}, u32[]{:S(2)}) copy-start(s32[1024]{0:T(1024)S(1)} %pad_clamp_fusion) | copy-start | bytes 12292
  2.6 29.8 %collective-permute-start = (f32[1,3,64]{2,1,0:T(4,128)S(1)}, f32[1,3,64]{2,1,0:T(4,128)S(1)}, u32[]{:S(2)}, u32[]{:S(2)}) collective-permute-start(f32[1,3,64]{2,1,0:T(4,128)S(1)} %get-tuple-element.590), channel_id=1, source_target_pairs={{0,4},{4,8},{8,12},{12,16},{16,20},{20,24},{24,28},{1,5},{5,9},{9,... | collective-permute-start | bytes 2312 | tf_op jit(solution)/shard_map/ppermute | solution.py:51
  7.5 24.9 %collective-permute-start.1 = (f32[1,3,64]{2,1,0:T(4,128)S(1)}, f32[1,3,64]{2,1,0:T(4,128)S(1)}, u32[]{:S(2)}, u32[]{:S(2)}) collective-permute-start(f32[1,3,64]{2,1,0:T(4,128)S(1)} %get-tuple-element.591), channel_id=1, source_target_pairs={{4,0},{8,4},{12,8},{16,12},{20,16},{24,20},{28,24},{5,1},{9,5},{13... | collective-permute-start | bytes 2312 | tf_op jit(solution)/shard_map/ppermute | solution.py:53
  10.5 7.5 %copy-start = (f32[128,9,128]{2,0,1:T(8,128)S(1)}, f32[128,9,128]{2,0,1:T(8,128)}, u32[]{:S(2)}) copy-start(f32[128,9,128]{2,0,1:T(8,128)} %param.6) | copy-start | bytes 1769476
  10.5 7.5 %copy-start.57 = (s32[2,3]{1,0:T(2,128)S(1)}, s32[2,3]{1,0:T(2,128)}, u32[]{:S(2)}) copy-start(s32[2,3]{1,0:T(2,128)} %param.10) | copy-start | bytes 76
  10.5 9.5 %copy-start.55 = (f32[2,8,128]{2,1,0:T(8,128)S(1)}, f32[2,8,128]{2,1,0:T(8,128)}, u32[]{:S(2)}) copy-start(f32[2,8,128]{2,1,0:T(8,128)} %param.9) | copy-start | bytes 24580
  11.3 38.5 %collective-permute-start.2 = (bf16[1,64,9,128]{3,1,2,0:T(8,128)(2,1)}, bf16[1,64,9,128]{3,1,2,0:T(8,128)(2,1)}, u32[]{:S(2)}, u32[]{:S(2)}) collective-permute-start(bf16[1,64,9,128]{3,1,2,0:T(8,128)(2,1)} %get-tuple-element.509), channel_id=1, source_target_pairs={{0,4},{4,8},{8,12},{12,16},{16,20},{20,24},{24,28},{1,5},{5,9},{9,... | collective-permute-start | bytes 442376 | tf_op jit(solution)/shard_map/ppermute | solution.py:51
  16.5 33.4 %collective-permute-start.3 = (bf16[1,64,9,128]{3,1,2,0:T(8,128)(2,1)}, bf16[1,64,9,128]{3,1,2,0:T(8,128)(2,1)}, u32[]{:S(2)}, u32[]{:S(2)}) collective-permute-start(bf16[1,64,9,128]{3,1,2,0:T(8,128)(2,1)} %get-tuple-element.510), channel_id=1, source_target_pairs={{4,0},{8,4},{12,8},{16,12},{20,16},{24,20},{28,24},{5,1},{9,5},{13... | collective-permute-start | bytes 442376 | tf_op jit(solution)/shard_map/ppermute | solution.py:53
  34.1 2.0 %copy-start.9 = (bf16[1,8,32,64]{3,2,1,0:T(8,128)(2,1)}, bf16[1,8,32,64]{3,2,1,0:T(8,128)(2,1)S(1)}, u32[]{:S(2)}) copy-start(bf16[1,8,32,64]{3,2,1,0:T(8,128)(2,1)S(1)} %get-tuple-element.487) | copy-start | bytes 98308
  34.1 5.9 %copy-start.7 = (bf16[1,8,32,64]{3,2,1,0:T(8,128)(2,1)}, bf16[1,8,32,64]{3,2,1,0:T(8,128)(2,1)S(1)}, u32[]{:S(2)}) copy-start(bf16[1,8,32,64]{3,2,1,0:T(8,128)(2,1)S(1)} %get-tuple-element.480) | copy-start | bytes 98308
  34.1 6.5 %copy-start.11 = (bf16[1,8,32,64]{3,2,1,0:T(8,128)(2,1)}, bf16[1,8,32,64]{3,2,1,0:T(8,128)(2,1)S(1)}, u32[]{:S(2)}) copy-start(bf16[1,8,32,64]{3,2,1,0:T(8,128)(2,1)S(1)} %get-tuple-element.486) | copy-start | bytes 98308
  35.1 1.7 %copy-start.17 = (bf16[1,8,32,64]{3,2,1,0:T(8,128)(2,1)}, bf16[1,8,32,64]{3,2,1,0:T(8,128)(2,1)S(1)}, u32[]{:S(2)}) copy-start(bf16[1,8,32,64]{3,2,1,0:T(8,128)(2,1)S(1)} %get-tuple-element.488) | copy-start | bytes 98308
  35.1 2.3 %copy-start.15 = (bf16[1,8,32,64]{3,2,1,0:T(8,128)(2,1)}, bf16[1,8,32,64]{3,2,1,0:T(8,128)(2,1)S(1)}, u32[]{:S(2)}) copy-start(bf16[1,8,32,64]{3,2,1,0:T(8,128)(2,1)S(1)} %get-tuple-element.494) | copy-start | bytes 98308
  35.1 3.0 %copy-start.19 = (bf16[1,8,32,64]{3,2,1,0:T(8,128)(2,1)}, bf16[1,8,32,64]{3,2,1,0:T(8,128)(2,1)S(1)}, u32[]{:S(2)}) copy-start(bf16[1,8,32,64]{3,2,1,0:T(8,128)(2,1)S(1)} %get-tuple-element.495) | copy-start | bytes 98308
  35.3 1.5 copy-start.1
  36.1 5.4 %copy-start.13 = (bf16[1,8,32,64]{3,2,1,0:T(8,128)(2,1)}, bf16[1,8,32,64]{3,2,1,0:T(8,128)(2,1)S(1)}, u32[]{:S(2)}) copy-start(bf16[1,8,32,64]{3,2,1,0:T(8,128)(2,1)S(1)} %get-tuple-element.503) | copy-start | bytes 98308
  36.1 5.4 %copy-start.21 = (bf16[1,8,32,64]{3,2,1,0:T(8,128)(2,1)}, bf16[1,8,32,64]{3,2,1,0:T(8,128)(2,1)S(1)}, u32[]{:S(2)}) copy-start(bf16[1,8,32,64]{3,2,1,0:T(8,128)(2,1)S(1)} %get-tuple-element.502) | copy-start | bytes 98308
  41.9 0.7 copy-start.32
  42.6 0.9 copy-start.33
  50.9 1.1 copy-start.2
  50.9 1.1 copy-start.51
  50.9 1.3 copy-start.39
  51.0 1.9 %copy-start.49 = (f32[8,128]{1,0:T(8,128)S(1)}, f32[8,128]{1,0:T(8,128)}, u32[]{:S(2)}) copy-start(f32[8,128]{1,0:T(8,128)} %get-tuple-element.532) | copy-start | bytes 12292
  52.0 1.2 copy-start.37
  53.2 1.2 copy-start.53
  59.0 1.0 copy-start.20
  59.0 1.0 copy-start.31
  59.3 0.9 copy-start.16
  59.3 0.9 copy-start.18
  59.8 0.9 copy-start.30
  59.9 1.0 copy-start.29
  60.2 0.9 copy-start.23
  60.2 0.9 copy-start.28
  60.2 1.1 copy-start.14
  60.2 1.1 copy-start.22
  60.9 0.9 copy-start.27
  61.1 0.9 copy-start.12
  61.1 0.9 copy-start.25
  61.3 0.9 copy-start.8
  61.3 0.9 copy-start.10
  61.7 0.9 copy-start.26
  61.9 0.9 copy-start.24
  62.2 1.0 copy-start.4
  62.6 1.0 copy-start.5
  63.0 1.0 copy-start.6
  63.3 0.9 copy-start.36
  63.6 0.7 copy-start.34
  63.6 0.7 copy-start.35
  64.7 0.9 copy-start.3
  72.5 8.2 %collective-permute-start.4 = (bf16[1,64,9,128]{3,1,2,0:T(8,128)(2,1)S(1)}, bf16[1,64,9,128]{3,1,2,0:T(8,128)(2,1)S(1)}, u32[]{:S(2)}, u32[]{:S(2)}) collective-permute-start(bf16[1,64,9,128]{3,1,2,0:T(8,128)(2,1)S(1)} %get-tuple-element.508), channel_id=1, source_target_pairs={{0,4},{4,8},{8,12},{12,16},{16,20},{20,24},{24,28},{1,5},{5,9},{9,... | collective-permute-start | bytes 442376 | tf_op jit(solution)/shard_map/ppermute | solution.py:51
  77.1 8.7 %collective-permute-start.5 = (bf16[1,64,9,128]{3,1,2,0:T(8,128)(2,1)S(1)}, bf16[1,64,9,128]{3,1,2,0:T(8,128)(2,1)S(1)}, u32[]{:S(2)}, u32[]{:S(2)}) collective-permute-start(bf16[1,64,9,128]{3,1,2,0:T(8,128)(2,1)S(1)} %get-tuple-element.507), channel_id=1, source_target_pairs={{4,0},{8,4},{12,8},{16,12},{20,16},{24,20},{28,24},{5,1},{9,5},{13... | collective-permute-start | bytes 442376 | tf_op jit(solution)/shard_map/ppermute | solution.py:53
  97.1 0.9 copy-start.52
  97.2 0.9 copy-start.54
  98.0 0.7 copy-start.40
  98.1 0.7 copy-start.48
  98.8 0.7 copy-start.47
  99.5 0.7 copy-start.46
  100.2 0.7 copy-start.50
  100.9 0.7 copy-start.38
  100.9 0.7 copy-start.45
  101.4 0.7 copy-start.43
  101.4 0.7 copy-start.44
  102.1 0.7 copy-start.41
  102.1 0.7 copy-start.42
